TPU v7x, 256 devices: a whole 4x4x8 slice. The times are simulated.
256 devices in a mesh: leaf: 64 (over z, x, core), sub: 4 (over y).
Axes of the slice: x: 4, y: 4, z: 8, core: 2. Of those that a mesh axis runs over, the one named last changes fastest.
Arguments:
- coords: bfloat16 [32768, 3, 128], P('leaf'), may hold values from 0 to 4
- charges: bfloat16 [32768, 8, 128], P(('leaf', 'sub')), may hold values from -6 to 6
- counts: int32 [32768], P('leaf'), may hold values from 32 to 128, as said below
- morton: int32 [32768], P('leaf'), may hold values from 0 to 511, as said below
- near_list: int32 [32768, 27], P(('leaf', 'sub')), may hold values from -1 to 32767, as said below
- basis: bfloat16 [32768, 64, 128], P(('leaf', 'sub')), may hold values from -0.5 to 0.5
- transfer1: bfloat16 [32768, 64, 64], P(('leaf', 'sub')), may hold values from -0.75 to 0.75
- far2_list: int32 [4096, 16], P(('leaf', 'sub')), may hold values from -1 to 4095, as said below
- coupling2: bfloat16 [4096, 16, 64, 64], P(('leaf', 'sub')), may hold values from -0.0625 to 0.0625
- transfer2: bfloat16 [4096, 64, 64], P('leaf'), may hold values from -0.75 to 0.75
- far3_list: int32 [64, 8], P('leaf'), may hold values from -1 to 63, as said below
- coupling3: bfloat16 [64, 8, 64, 64], P('leaf'), may hold values from -0.01171875 to 0.01171875
Outputs:
- potential: float32 [32768, 8, 128], P(('leaf', 'sub'))
Inputs may be any that keep to these rules, and one draw needn't show every extreme that they name: `counts`: each leaf's number of live points; leaves do not all have the same number. `morton`: within every block of 512 consecutive entries, a permutation of 0 to 511. `near_list`: row t starts with t itself; its other live entries are leaves other than t in the leaf group of t or in the group just before or after it; live entries come first and -1 fills the rest, with at least 13 live entries a row; entries may repeat. `far2_list`: row b names boxes other than b in the leaf group of b or in the group just before or after it; live entries come first and -1 fills the rest, with at least 8 live entries a row; entries may repeat. `far3_list`: row q names group boxes other than q; live entries come first and -1 fills the rest, with at least 4 live entries a row; entries may repeat.
All inputs are finite; a program needn't handle non-finite values.
Results may differ from a plain program's by a relative error of at most 0.011.
Values may be sent and summed in bfloat16 or wider, within the bound.
No kernel may reach another device: no remote copies, remote signals or barrier semaphores. Data moves between devices by JAX's collectives and lax.ppermute only.
A program may use at most 64 MiB of HBM per device.

v0:
```python
import jax
import jax.numpy as jnp
from jax import lax
from jax.sharding import PartitionSpec as P

kernel_scale = 0.07957747154594767
delta_squared = 0.0025


def with_halo(cells, sides, width):
    for axis, dim in sides:
        count = lax.axis_size(axis)
        ends = count - 1
        head = lax.slice_in_dim(cells, 0, width, axis=dim)
        tail = lax.slice_in_dim(cells, cells.shape[dim] - width, cells.shape[dim], axis=dim)
        cells = jnp.concatenate(
            [
                lax.ppermute(tail, axis, [(i, (i + 1) % count) for i in range(ends)]),
                cells,
                lax.ppermute(head, axis, [((i + 1) % count, i) for i in range(ends)]),
            ],
            axis=dim,
        )
    return cells


def kernel_tile(targets, sources):
    squared = jnp.zeros((targets.shape[0], targets.shape[2], sources.shape[2]), jnp.float32)
    for component in range(3):
        offset = targets[:, component, :, None] - sources[:, component, None, :]
        squared = squared + offset * offset
    return (kernel_scale / jnp.sqrt(squared + delta_squared)).astype(jnp.bfloat16)


def far_field(moments, lists, couplings, offset):
    valid = lists >= 0
    local = jnp.clip(lists - offset, 0, moments.shape[0] - 1)
    source = jnp.where(valid[..., None, None], moments[local], jnp.zeros((), moments.dtype))
    return jnp.einsum("bkrc,bkcp->brp", source, couplings, preferred_element_type=jnp.float32)


def on_device(
    coords,
    charges,
    counts,
    morton,
    near_list,
    basis,
    transfer1,
    far2_list,
    coupling2,
    transfer2,
    far3_list,
    coupling3,
):
    lane = lax.axis_index("sub")
    group = lax.axis_index("leaf")
    leaf_dev = charges.shape[0]
    rhs_count = charges.shape[1]
    points = charges.shape[2]
    rank_size = basis.shape[1]
    group_size = coords.shape[0]
    clusters = far2_list.shape[0]
    group_boxes = transfer2.shape[0]
    start = lane * leaf_dev
    arrived = lax.all_gather(charges, "sub", axis=0, tiled=True)
    inverse = (
        jnp.zeros((group_size,), jnp.int32).at[morton].set(jnp.arange(group_size, dtype=jnp.int32))
    )
    ordered = arrived[inverse]
    live = jnp.arange(points, dtype=jnp.int32)[None, :] < counts[:, None]
    masked = jnp.where(live[:, None, :], ordered, jnp.zeros((), ordered.dtype))
    packed = jnp.concatenate([coords, masked], axis=1)
    nearby = with_halo(packed, (("leaf", 0),), group_size)
    own_charges = lax.dynamic_slice_in_dim(masked, start, leaf_dev, 0)
    own_live = lax.dynamic_slice_in_dim(live, start, leaf_dev, 0)
    targets = lax.dynamic_slice_in_dim(coords, start, leaf_dev, 0).astype(jnp.float32)
    transfer_boxed = transfer1.reshape(clusters, 8, rank_size, rank_size)
    leaf_moments = jnp.einsum(
        "trp,tkp->trk", own_charges, basis, preferred_element_type=jnp.float32
    ).astype(jnp.bfloat16)
    box_moments = jnp.einsum(
        "bnrc,bncp->brp",
        leaf_moments.reshape(clusters, 8, rhs_count, rank_size),
        transfer_boxed,
        preferred_element_type=jnp.float32,
    ).astype(jnp.bfloat16)
    group_moments = lax.all_gather(box_moments, "sub", axis=0, tiled=True)
    top_moment = jnp.einsum(
        "brc,bcp->rp", group_moments, transfer2, preferred_element_type=jnp.float32
    ).astype(jnp.bfloat16)
    all_top = lax.all_gather(top_moment[None], "leaf", axis=0, tiled=True)
    near_boxes = with_halo(group_moments, (("leaf", 0),), group_boxes)
    top_field = far_field(all_top, far3_list, coupling3, 0).astype(jnp.bfloat16)
    box_far = far_field(near_boxes, far2_list, coupling2, (group - 1) * group_boxes)
    own_transfer = lax.dynamic_slice_in_dim(transfer2, lane * clusters, clusters, 0)
    box_local = (
        box_far
        + jnp.einsum("rp,bcp->brc", top_field[0], own_transfer, preferred_element_type=jnp.float32)
    ).astype(jnp.bfloat16)
    leaf_local = jnp.einsum(
        "brp,bncp->bnrc", box_local, transfer_boxed, preferred_element_type=jnp.float32
    ).astype(jnp.bfloat16)
    leaf_local = leaf_local.reshape(leaf_dev, rhs_count, rank_size)
    far_part = jnp.einsum("trk,tkp->trp", leaf_local, basis, preferred_element_type=jnp.float32)
    base = (group - 1) * group_size

    def slot_step(total, column):
        valid = column >= 0
        index = jnp.clip(column - base, 0, 3 * group_size - 1)
        rows = nearby[index]
        tile = kernel_tile(targets, rows[:, :3].astype(jnp.float32))
        source = jnp.where(valid[:, None, None], rows[:, 3:], jnp.zeros((), rows.dtype))
        return (
            total + jnp.einsum("tij,trj->tri", tile, source, preferred_element_type=jnp.float32),
            None,
        )

    near_part, unused = lax.scan(
        slot_step, jnp.zeros((leaf_dev, rhs_count, points), jnp.float32), near_list.T
    )
    return jnp.where(own_live[:, None, :], near_part + far_part, jnp.zeros((), jnp.float32))


def solution(mesh):
    return jax.shard_map(
        on_device,
        mesh=mesh,
        in_specs=(
            P("leaf", None, None),
            P(("leaf", "sub"), None, None),
            P("leaf"),
            P("leaf"),
            P(("leaf", "sub"), None),
            P(("leaf", "sub"), None, None),
            P(("leaf", "sub"), None, None),
            P(("leaf", "sub"), None),
            P(("leaf", "sub"), None, None, None),
            P("leaf", None, None),
            P("leaf", None),
            P("leaf", None, None, None),
        ),
        out_specs=P(("leaf", "sub"), None, None),
        check_vma=False,
    )
```

profile of v0, /device:TPU:1, one launch (start us, length us, event | category | flops | bytes accessed | tf_op | source)
XLA Modules:
  0.0 683.8 jit_solution(16244068060757462938)
XLA Ops:
  11.1 4.8 copy.23
  19.3 19.4 %all-gather.3.cloned.1.call-done = bf16[512,8,128]{2,1,0:T(8,128)(2,1)} async-done(((bf16[128,8,128]{2,1,0:T(8,128)(2,1)}), bf16[512,8,128]{2,1,0:T(8,128)(2,1)}) %all-gather.3.cloned.1.call-update) | async-done | bytes 1048592 | tf_op jit(solution)/shard_map/all_gather | solution.py:66
  45.3 9.5 %all_gather.10 = bf16[64,8,64]{2,1,0:T(8,128)(2,1)S(1)} all-gather(bf16[16,8,64]{2,1,0:T(8,128)(2,1)S(1)} %fusion.10), channel_id=1, replica_groups=mesh['leaf'=64,'sub'=4] {'sub'}, dimensions={0}, use_global_device_ids=true | all-gather | bytes 81920 | tf_op jit(solution)/shard_map/all_gather | solution.py:88
  54.8 7.1 %collective-permute-start.2 = (bf16[64,8,64]{2,1,0:T(8,128)(2,1)S(1)}, bf16[64,8,64]{2,1,0:T(8,128)(2,1)}, u32[]{:S(2)}, u32[]{:S(2)}) collective-permute-start(bf16[64,8,64]{2,1,0:T(8,128)(2,1)S(1)} %all_gather.10), channel_id=1, source_target_pairs={{0,4},{4,8},{8,12},{12,16},{16,20},{20,24},{24,28},{28,32},{32,36}... | collective-permute-start | bytes 196616 | tf_op jit(solution)/shard_map/ppermute | solution.py:18
  66.2 3.6 collective-permute-start
  72.1 72.7 %all-gather = bf16[512,64]{1,0:T(8,128)(2,1)} all-gather(bf16[8,64]{1,0:T(8,128)(2,1)S(1)} %fusion.12), channel_id=2, replica_groups=mesh['leaf'=64,'sub'=4] {'leaf'}, dimensions={0}, use_global_device_ids=true | all-gather | bytes 66560 | tf_op jit(solution)/shard_map/all_gather | solution.py:92
  151.8 3.5 convolution_bitcast_fusion.1
  155.4 4.3 convolution_convert_fusion
  167.0 25.8 %pad_maximum_fusion = bf16[1536,11,128]{2,1,0:T(8,128)(2,1)} fusion(bf16[512,11,128]{2,1,0:T(8,128)(2,1)S(1)} %copy.22, bf16[512,8,128]{2,1,0:T(8,128)(2,1)S(1)} %broadcast_select_fusion, bf16[512,3,128]{2,1,0:T(4,128)(2,1)S(1)} %copy-done.3, bf16[512,11,128]{2,1,0:T(8,128)(2,1)S(1)} %copy.21), kind=kLoop, calls=%fused_computation.23 | loop fusion | flops 17301504 | bytes 8650752 | tf_op jit(solution)/shard_map/concatenate | solution.py:16
  192.7 482.2 %while.11 = (s32[]{:T(128)}, f32[128,8,128]{2,1,0:T(8,128)}, s32[27,128]{1,0:T(8,128)}, s32[]{:T(128)}, bf16[1536,11,128]{2,1,0:T(8,128)(2,1)}, /*index=5*/f32[128,3,128]{2,0,1:T(8,128)S(1)}, s32[]{:T(128)}, s32[]{:T(128)}) while((s32[]{:T(128)}, f32[128,8,128]{2,1,0:T(8,128)}, s32[27,128]{1,0:T(8,128)}, s32[]{:T(128)}, ...), condition=%wide.region_2.3_spmd.clone, body=%wide.region_1.2_spmd.clone.sunk | while | flops 57067264 | bytes 3513195 | solution.py:119
  193.5 3.5 gather_fusion
  199.1 11.5 %fusion.50 = f32[128,8,128]{2,1,0:T(8,128)} fusion(f32[128,128]{1,0:T(8,128)S(1)} %bitcast.93, f32[128,128]{1,0:T(8,128)} %get-tuple-element.121, f32[128,128]{1,0:T(8,128)S(1)} %bitcast.94, f32[128,128]{1,0:T(8,128)} %get-tuple-element.123, f32[128,128]{1,0:T(8,128)S(1)} %bitcast.92, f32[128,128]{1,0:T(8,128)} %get-tuple-element.125, ...), kind=kOutput, calls=%fused_computation.7.clone.1 | convolution fusion | flops 57016320 | bytes 1704065 | tf_op jit(solution)/shard_map/while/body/eval_jaxpr/tij,trj->tri/dot_general | solution.py:115
  211.3 3.5 gather_fusion
  216.9 11.6 %fusion.50 = f32[128,8,128]{2,1,0:T(8,128)} fusion(f32[128,128]{1,0:T(8,128)S(1)} %bitcast.93, f32[128,128]{1,0:T(8,128)} %get-tuple-element.121, f32[128,128]{1,0:T(8,128)S(1)} %bitcast.94, f32[128,128]{1,0:T(8,128)} %get-tuple-element.123, f32[128,128]{1,0:T(8,128)S(1)} %bitcast.92, f32[128,128]{1,0:T(8,128)} %get-tuple-element.125, ...), kind=kOutput, calls=%fused_computation.7.clone.1 | convolution fusion | flops 57016320 | bytes 1704065 | tf_op jit(solution)/shard_map/while/body/eval_jaxpr/tij,trj->tri/dot_general | solution.py:115
  229.2 3.5 gather_fusion
  234.7 11.6 %fusion.50 = f32[128,8,128]{2,1,0:T(8,128)} fusion(f32[128,128]{1,0:T(8,128)S(1)} %bitcast.93, f32[128,128]{1,0:T(8,128)} %get-tuple-element.121, f32[128,128]{1,0:T(8,128)S(1)} %bitcast.94, f32[128,128]{1,0:T(8,128)} %get-tuple-element.123, f32[128,128]{1,0:T(8,128)S(1)} %bitcast.92, f32[128,128]{1,0:T(8,128)} %get-tuple-element.125, ...), kind=kOutput, calls=%fused_computation.7.clone.1 | convolution fusion | flops 57016320 | bytes 1704065 | tf_op jit(solution)/shard_map/while/body/eval_jaxpr/tij,trj->tri/dot_general | solution.py:115
  252.6 11.6 %fusion.50 = f32[128,8,128]{2,1,0:T(8,128)} fusion(f32[128,128]{1,0:T(8,128)S(1)} %bitcast.93, f32[128,128]{1,0:T(8,128)} %get-tuple-element.121, f32[128,128]{1,0:T(8,128)S(1)} %bitcast.94, f32[128,128]{1,0:T(8,128)} %get-tuple-element.123, f32[128,128]{1,0:T(8,128)S(1)} %bitcast.92, f32[128,128]{1,0:T(8,128)} %get-tuple-element.125, ...), kind=kOutput, calls=%fused_computation.7.clone.1 | convolution fusion | flops 57016320 | bytes 1704065 | tf_op jit(solution)/shard_map/while/body/eval_jaxpr/tij,trj->tri/dot_general | solution.py:115
  270.5 11.6 %fusion.50 = f32[128,8,128]{2,1,0:T(8,128)} fusion(f32[128,128]{1,0:T(8,128)S(1)} %bitcast.93, f32[128,128]{1,0:T(8,128)} %get-tuple-element.121, f32[128,128]{1,0:T(8,128)S(1)} %bitcast.94, f32[128,128]{1,0:T(8,128)} %get-tuple-element.123, f32[128,128]{1,0:T(8,128)S(1)} %bitcast.92, f32[128,128]{1,0:T(8,128)} %get-tuple-element.125, ...), kind=kOutput, calls=%fused_computation.7.clone.1 | convolution fusion | flops 57016320 | bytes 1704065 | tf_op jit(solution)/shard_map/while/body/eval_jaxpr/tij,trj->tri/dot_general | solution.py:115
  282.7 3.5 gather_fusion
  288.3 11.6 %fusion.50 = f32[128,8,128]{2,1,0:T(8,128)} fusion(f32[128,128]{1,0:T(8,128)S(1)} %bitcast.93, f32[128,128]{1,0:T(8,128)} %get-tuple-element.121, f32[128,128]{1,0:T(8,128)S(1)} %bitcast.94, f32[128,128]{1,0:T(8,128)} %get-tuple-element.123, f32[128,128]{1,0:T(8,128)S(1)} %bitcast.92, f32[128,128]{1,0:T(8,128)} %get-tuple-element.125, ...), kind=kOutput, calls=%fused_computation.7.clone.1 | convolution fusion | flops 57016320 | bytes 1704065 | tf_op jit(solution)/shard_map/while/body/eval_jaxpr/tij,trj->tri/dot_general | solution.py:115
  300.6 3.5 gather_fusion
  306.2 11.6 %fusion.50 = f32[128,8,128]{2,1,0:T(8,128)} fusion(f32[128,128]{1,0:T(8,128)S(1)} %bitcast.93, f32[128,128]{1,0:T(8,128)} %get-tuple-element.121, f32[128,128]{1,0:T(8,128)S(1)} %bitcast.94, f32[128,128]{1,0:T(8,128)} %get-tuple-element.123, f32[128,128]{1,0:T(8,128)S(1)} %bitcast.92, f32[128,128]{1,0:T(8,128)} %get-tuple-element.125, ...), kind=kOutput, calls=%fused_computation.7.clone.1 | convolution fusion | flops 57016320 | bytes 1704065 | tf_op jit(solution)/shard_map/while/body/eval_jaxpr/tij,trj->tri/dot_general | solution.py:115
  318.5 3.5 gather_fusion
  324.1 11.6 %fusion.50 = f32[128,8,128]{2,1,0:T(8,128)} fusion(f32[128,128]{1,0:T(8,128)S(1)} %bitcast.93, f32[128,128]{1,0:T(8,128)} %get-tuple-element.121, f32[128,128]{1,0:T(8,128)S(1)} %bitcast.94, f32[128,128]{1,0:T(8,128)} %get-tuple-element.123, f32[128,128]{1,0:T(8,128)S(1)} %bitcast.92, f32[128,128]{1,0:T(8,128)} %get-tuple-element.125, ...), kind=kOutput, calls=%fused_computation.7.clone.1 | convolution fusion | flops 57016320 | bytes 1704065 | tf_op jit(solution)/shard_map/while/body/eval_jaxpr/tij,trj->tri/dot_general | solution.py:115
  341.9 11.6 %fusion.50 = f32[128,8,128]{2,1,0:T(8,128)} fusion(f32[128,128]{1,0:T(8,128)S(1)} %bitcast.93, f32[128,128]{1,0:T(8,128)} %get-tuple-element.121, f32[128,128]{1,0:T(8,128)S(1)} %bitcast.94, f32[128,128]{1,0:T(8,128)} %get-tuple-element.123, f32[128,128]{1,0:T(8,128)S(1)} %bitcast.92, f32[128,128]{1,0:T(8,128)} %get-tuple-element.125, ...), kind=kOutput, calls=%fused_computation.7.clone.1 | convolution fusion | flops 57016320 | bytes 1704065 | tf_op jit(solution)/shard_map/while/body/eval_jaxpr/tij,trj->tri/dot_general | solution.py:115
  359.8 11.6 %fusion.50 = f32[128,8,128]{2,1,0:T(8,128)} fusion(f32[128,128]{1,0:T(8,128)S(1)} %bitcast.93, f32[128,128]{1,0:T(8,128)} %get-tuple-element.121, f32[128,128]{1,0:T(8,128)S(1)} %bitcast.94, f32[128,128]{1,0:T(8,128)} %get-tuple-element.123, f32[128,128]{1,0:T(8,128)S(1)} %bitcast.92, f32[128,128]{1,0:T(8,128)} %get-tuple-element.125, ...), kind=kOutput, calls=%fused_computation.7.clone.1 | convolution fusion | flops 57016320 | bytes 1704065 | tf_op jit(solution)/shard_map/while/body/eval_jaxpr/tij,trj->tri/dot_general | solution.py:115
  372.1 3.5 gather_fusion
  377.6 11.6 %fusion.50 = f32[128,8,128]{2,1,0:T(8,128)} fusion(f32[128,128]{1,0:T(8,128)S(1)} %bitcast.93, f32[128,128]{1,0:T(8,128)} %get-tuple-element.121, f32[128,128]{1,0:T(8,128)S(1)} %bitcast.94, f32[128,128]{1,0:T(8,128)} %get-tuple-element.123, f32[128,128]{1,0:T(8,128)S(1)} %bitcast.92, f32[128,128]{1,0:T(8,128)} %get-tuple-element.125, ...), kind=kOutput, calls=%fused_computation.7.clone.1 | convolution fusion | flops 57016320 | bytes 1704065 | tf_op jit(solution)/shard_map/while/body/eval_jaxpr/tij,trj->tri/dot_general | solution.py:115
  389.9 3.5 gather_fusion
  395.5 11.6 %fusion.50 = f32[128,8,128]{2,1,0:T(8,128)} fusion(f32[128,128]{1,0:T(8,128)S(1)} %bitcast.93, f32[128,128]{1,0:T(8,128)} %get-tuple-element.121, f32[128,128]{1,0:T(8,128)S(1)} %bitcast.94, f32[128,128]{1,0:T(8,128)} %get-tuple-element.123, f32[128,128]{1,0:T(8,128)S(1)} %bitcast.92, f32[128,128]{1,0:T(8,128)} %get-tuple-element.125, ...), kind=kOutput, calls=%fused_computation.7.clone.1 | convolution fusion | flops 57016320 | bytes 1704065 | tf_op jit(solution)/shard_map/while/body/eval_jaxpr/tij,trj->tri/dot_general | solution.py:115
  407.8 3.5 gather_fusion
  413.4 11.6 %fusion.50 = f32[128,8,128]{2,1,0:T(8,128)} fusion(f32[128,128]{1,0:T(8,128)S(1)} %bitcast.93, f32[128,128]{1,0:T(8,128)} %get-tuple-element.121, f32[128,128]{1,0:T(8,128)S(1)} %bitcast.94, f32[128,128]{1,0:T(8,128)} %get-tuple-element.123, f32[128,128]{1,0:T(8,128)S(1)} %bitcast.92, f32[128,128]{1,0:T(8,128)} %get-tuple-element.125, ...), kind=kOutput, calls=%fused_computation.7.clone.1 | convolution fusion | flops 57016320 | bytes 1704065 | tf_op jit(solution)/shard_map/while/body/eval_jaxpr/tij,trj->tri/dot_general | solution.py:115
  425.7 3.5 gather_fusion
  431.2 11.6 %fusion.50 = f32[128,8,128]{2,1,0:T(8,128)} fusion(f32[128,128]{1,0:T(8,128)S(1)} %bitcast.93, f32[128,128]{1,0:T(8,128)} %get-tuple-element.121, f32[128,128]{1,0:T(8,128)S(1)} %bitcast.94, f32[128,128]{1,0:T(8,128)} %get-tuple-element.123, f32[128,128]{1,0:T(8,128)S(1)} %bitcast.92, f32[128,128]{1,0:T(8,128)} %get-tuple-element.125, ...), kind=kOutput, calls=%fused_computation.7.clone.1 | convolution fusion | flops 57016320 | bytes 1704065 | tf_op jit(solution)/shard_map/while/body/eval_jaxpr/tij,trj->tri/dot_general | solution.py:115
  449.1 11.6 %fusion.50 = f32[128,8,128]{2,1,0:T(8,128)} fusion(f32[128,128]{1,0:T(8,128)S(1)} %bitcast.93, f32[128,128]{1,0:T(8,128)} %get-tuple-element.121, f32[128,128]{1,0:T(8,128)S(1)} %bitcast.94, f32[128,128]{1,0:T(8,128)} %get-tuple-element.123, f32[128,128]{1,0:T(8,128)S(1)} %bitcast.92, f32[128,128]{1,0:T(8,128)} %get-tuple-element.125, ...), kind=kOutput, calls=%fused_computation.7.clone.1 | convolution fusion | flops 57016320 | bytes 1704065 | tf_op jit(solution)/shard_map/while/body/eval_jaxpr/tij,trj->tri/dot_general | solution.py:115
  467.0 11.6 %fusion.50 = f32[128,8,128]{2,1,0:T(8,128)} fusion(f32[128,128]{1,0:T(8,128)S(1)} %bitcast.93, f32[128,128]{1,0:T(8,128)} %get-tuple-element.121, f32[128,128]{1,0:T(8,128)S(1)} %bitcast.94, f32[128,128]{1,0:T(8,128)} %get-tuple-element.123, f32[128,128]{1,0:T(8,128)S(1)} %bitcast.92, f32[128,128]{1,0:T(8,128)} %get-tuple-element.125, ...), kind=kOutput, calls=%fused_computation.7.clone.1 | convolution fusion | flops 57016320 | bytes 1704065 | tf_op jit(solution)/shard_map/while/body/eval_jaxpr/tij,trj->tri/dot_general | solution.py:115
  484.8 11.6 %fusion.50 = f32[128,8,128]{2,1,0:T(8,128)} fusion(f32[128,128]{1,0:T(8,128)S(1)} %bitcast.93, f32[128,128]{1,0:T(8,128)} %get-tuple-element.121, f32[128,128]{1,0:T(8,128)S(1)} %bitcast.94, f32[128,128]{1,0:T(8,128)} %get-tuple-element.123, f32[128,128]{1,0:T(8,128)S(1)} %bitcast.92, f32[128,128]{1,0:T(8,128)} %get-tuple-element.125, ...), kind=kOutput, calls=%fused_computation.7.clone.1 | convolution fusion | flops 57016320 | bytes 1704065 | tf_op jit(solution)/shard_map/while/body/eval_jaxpr/tij,trj->tri/dot_general | solution.py:115
  502.7 11.6 %fusion.50 = f32[128,8,128]{2,1,0:T(8,128)} fusion(f32[128,128]{1,0:T(8,128)S(1)} %bitcast.93, f32[128,128]{1,0:T(8,128)} %get-tuple-element.121, f32[128,128]{1,0:T(8,128)S(1)} %bitcast.94, f32[128,128]{1,0:T(8,128)} %get-tuple-element.123, f32[128,128]{1,0:T(8,128)S(1)} %bitcast.92, f32[128,128]{1,0:T(8,128)} %get-tuple-element.125, ...), kind=kOutput, calls=%fused_computation.7.clone.1 | convolution fusion | flops 57016320 | bytes 1704065 | tf_op jit(solution)/shard_map/while/body/eval_jaxpr/tij,trj->tri/dot_general | solution.py:115
  515.0 3.5 gather_fusion
  520.5 11.6 %fusion.50 = f32[128,8,128]{2,1,0:T(8,128)} fusion(f32[128,128]{1,0:T(8,128)S(1)} %bitcast.93, f32[128,128]{1,0:T(8,128)} %get-tuple-element.121, f32[128,128]{1,0:T(8,128)S(1)} %bitcast.94, f32[128,128]{1,0:T(8,128)} %get-tuple-element.123, f32[128,128]{1,0:T(8,128)S(1)} %bitcast.92, f32[128,128]{1,0:T(8,128)} %get-tuple-element.125, ...), kind=kOutput, calls=%fused_computation.7.clone.1 | convolution fusion | flops 57016320 | bytes 1704065 | tf_op jit(solution)/shard_map/while/body/eval_jaxpr/tij,trj->tri/dot_general | solution.py:115
  538.4 11.6 %fusion.50 = f32[128,8,128]{2,1,0:T(8,128)} fusion(f32[128,128]{1,0:T(8,128)S(1)} %bitcast.93, f32[128,128]{1,0:T(8,128)} %get-tuple-element.121, f32[128,128]{1,0:T(8,128)S(1)} %bitcast.94, f32[128,128]{1,0:T(8,128)} %get-tuple-element.123, f32[128,128]{1,0:T(8,128)S(1)} %bitcast.92, f32[128,128]{1,0:T(8,128)} %get-tuple-element.125, ...), kind=kOutput, calls=%fused_computation.7.clone.1 | convolution fusion | flops 57016320 | bytes 1704065 | tf_op jit(solution)/shard_map/while/body/eval_jaxpr/tij,trj->tri/dot_general | solution.py:115
  556.3 11.6 %fusion.50 = f32[128,8,128]{2,1,0:T(8,128)} fusion(f32[128,128]{1,0:T(8,128)S(1)} %bitcast.93, f32[128,128]{1,0:T(8,128)} %get-tuple-element.121, f32[128,128]{1,0:T(8,128)S(1)} %bitcast.94, f32[128,128]{1,0:T(8,128)} %get-tuple-element.123, f32[128,128]{1,0:T(8,128)S(1)} %bitcast.92, f32[128,128]{1,0:T(8,128)} %get-tuple-element.125, ...), kind=kOutput, calls=%fused_computation.7.clone.1 | convolution fusion | flops 57016320 | bytes 1704065 | tf_op jit(solution)/shard_map/while/body/eval_jaxpr/tij,trj->tri/dot_general | solution.py:115
  574.1 11.6 %fusion.50 = f32[128,8,128]{2,1,0:T(8,128)} fusion(f32[128,128]{1,0:T(8,128)S(1)} %bitcast.93, f32[128,128]{1,0:T(8,128)} %get-tuple-element.121, f32[128,128]{1,0:T(8,128)S(1)} %bitcast.94, f32[128,128]{1,0:T(8,128)} %get-tuple-element.123, f32[128,128]{1,0:T(8,128)S(1)} %bitcast.92, f32[128,128]{1,0:T(8,128)} %get-tuple-element.125, ...), kind=kOutput, calls=%fused_computation.7.clone.1 | convolution fusion | flops 57016320 | bytes 1704065 | tf_op jit(solution)/shard_map/while/body/eval_jaxpr/tij,trj->tri/dot_general | solution.py:115
  592.0 11.6 %fusion.50 = f32[128,8,128]{2,1,0:T(8,128)} fusion(f32[128,128]{1,0:T(8,128)S(1)} %bitcast.93, f32[128,128]{1,0:T(8,128)} %get-tuple-element.121, f32[128,128]{1,0:T(8,128)S(1)} %bitcast.94, f32[128,128]{1,0:T(8,128)} %get-tuple-element.123, f32[128,128]{1,0:T(8,128)S(1)} %bitcast.92, f32[128,128]{1,0:T(8,128)} %get-tuple-element.125, ...), kind=kOutput, calls=%fused_computation.7.clone.1 | convolution fusion | flops 57016320 | bytes 1704065 | tf_op jit(solution)/shard_map/while/body/eval_jaxpr/tij,trj->tri/dot_general | solution.py:115
  609.8 11.6 %fusion.50 = f32[128,8,128]{2,1,0:T(8,128)} fusion(f32[128,128]{1,0:T(8,128)S(1)} %bitcast.93, f32[128,128]{1,0:T(8,128)} %get-tuple-element.121, f32[128,128]{1,0:T(8,128)S(1)} %bitcast.94, f32[128,128]{1,0:T(8,128)} %get-tuple-element.123, f32[128,128]{1,0:T(8,128)S(1)} %bitcast.92, f32[128,128]{1,0:T(8,128)} %get-tuple-element.125, ...), kind=kOutput, calls=%fused_computation.7.clone.1 | convolution fusion | flops 57016320 | bytes 1704065 | tf_op jit(solution)/shard_map/while/body/eval_jaxpr/tij,trj->tri/dot_general | solution.py:115
  627.7 11.6 %fusion.50 = f32[128,8,128]{2,1,0:T(8,128)} fusion(f32[128,128]{1,0:T(8,128)S(1)} %bitcast.93, f32[128,128]{1,0:T(8,128)} %get-tuple-element.121, f32[128,128]{1,0:T(8,128)S(1)} %bitcast.94, f32[128,128]{1,0:T(8,128)} %get-tuple-element.123, f32[128,128]{1,0:T(8,128)S(1)} %bitcast.92, f32[128,128]{1,0:T(8,128)} %get-tuple-element.125, ...), kind=kOutput, calls=%fused_computation.7.clone.1 | convolution fusion | flops 57016320 | bytes 1704065 | tf_op jit(solution)/shard_map/while/body/eval_jaxpr/tij,trj->tri/dot_general | solution.py:115
  645.6 11.6 %fusion.50 = f32[128,8,128]{2,1,0:T(8,128)} fusion(f32[128,128]{1,0:T(8,128)S(1)} %bitcast.93, f32[128,128]{1,0:T(8,128)} %get-tuple-element.121, f32[128,128]{1,0:T(8,128)S(1)} %bitcast.94, f32[128,128]{1,0:T(8,128)} %get-tuple-element.123, f32[128,128]{1,0:T(8,128)S(1)} %bitcast.92, f32[128,128]{1,0:T(8,128)} %get-tuple-element.125, ...), kind=kOutput, calls=%fused_computation.7.clone.1 | convolution fusion | flops 57016320 | bytes 1704065 | tf_op jit(solution)/shard_map/while/body/eval_jaxpr/tij,trj->tri/dot_general | solution.py:115
  663.4 11.6 %fusion.50 = f32[128,8,128]{2,1,0:T(8,128)} fusion(f32[128,128]{1,0:T(8,128)S(1)} %bitcast.93, f32[128,128]{1,0:T(8,128)} %get-tuple-element.121, f32[128,128]{1,0:T(8,128)S(1)} %bitcast.94, f32[128,128]{1,0:T(8,128)} %get-tuple-element.123, f32[128,128]{1,0:T(8,128)S(1)} %bitcast.92, f32[128,128]{1,0:T(8,128)} %get-tuple-element.125, ...), kind=kOutput, calls=%fused_computation.7.clone.1 | convolution fusion | flops 57016320 | bytes 1704065 | tf_op jit(solution)/shard_map/while/body/eval_jaxpr/tij,trj->tri/dot_general | solution.py:115
  (236 shorter events, 168.1 us)
Async XLA Ops:
  6.5 37.1 %copy-start = (bf16[128,64,128]{2,1,0:T(8,128)(2,1)S(1)}, bf16[128,64,128]{2,1,0:T(8,128)(2,1)}, u32[]{:S(2)}) copy-start(bf16[128,64,128]{2,1,0:T(8,128)(2,1)} %param.19) | copy-start | bytes 6291460
  6.5 12.7 %copy-start.6 = (s32[16,16]{1,0:T(8,128)S(1)}, s32[16,16]{1,0:T(8,128)}, u32[]{:S(2)}) copy-start(s32[16,16]{1,0:T(8,128)} %param.21) | copy-start | bytes 3076
  6.5 11.6 %copy-start.8 = (s32[1,8]{1,0:T(1,128)S(1)}, s32[1,8]{1,0:T(1,128)}, u32[]{:S(2)}) copy-start(s32[1,8]{1,0:T(1,128)} %param.24) | copy-start | bytes 100
  6.5 11.6 %copy-start.7 = (s32[512]{0:T(512)S(1)}, s32[512]{0:T(512)}, u32[]{:S(2)}) copy-start(s32[512]{0:T(512)} %param.16) | copy-start | bytes 6148
  6.5 32.1 %all-gather.3.cloned.1.call-start = ((), (), s32[]{:S(2)}) async-start(), calls=%async_computation | async-start | bytes 1310720 | tf_op jit(solution)/shard_map/all_gather | solution.py:66
  42.0 2.9 copy-start.1
  42.0 21.9 %copy-start.2 = (bf16[512,3,128]{2,1,0:T(4,128)(2,1)S(1)}, bf16[512,3,128]{2,1,0:T(4,128)(2,1)}, u32[]{:S(2)}) copy-start(bf16[512,3,128]{2,1,0:T(4,128)(2,1)} %copy.18) | copy-start | bytes 1179652
  45.3 26.5 %copy-start.5 = (bf16[64,64,64]{2,1,0:T(8,128)(2,1)S(1)}, bf16[64,64,64]{2,1,0:T(8,128)(2,1)}, u32[]{:S(2)}) copy-start(bf16[64,64,64]{2,1,0:T(8,128)(2,1)} %param.23) | copy-start | bytes 1572868
  54.8 92.6 %collective-permute-start.2 = (bf16[64,8,64]{2,1,0:T(8,128)(2,1)S(1)}, bf16[64,8,64]{2,1,0:T(8,128)(2,1)}, u32[]{:S(2)}, u32[]{:S(2)}) collective-permute-start(bf16[64,8,64]{2,1,0:T(8,128)(2,1)S(1)} %all_gather.10), channel_id=1, source_target_pairs={{0,4},{4,8},{8,12},{12,16},{16,20},{20,24},{24,28},{28,32},{32,36}... | collective-permute-start | bytes 196616 | tf_op jit(solution)/shard_map/ppermute | solution.py:18
  62.0 85.5 %collective-permute-start.3 = (bf16[64,8,64]{2,1,0:T(8,128)(2,1)S(1)}, bf16[64,8,64]{2,1,0:T(8,128)(2,1)}, u32[]{:S(2)}, u32[]{:S(2)}) collective-permute-start(bf16[64,8,64]{2,1,0:T(8,128)(2,1)S(1)} %all_gather.10), channel_id=1, source_target_pairs={{4,0},{8,4},{12,8},{16,12},{20,16},{24,20},{28,24},{32,28},{36,32}... | collective-permute-start | bytes 196616 | tf_op jit(solution)/shard_map/ppermute | solution.py:20
  66.2 95.9 %collective-permute-start = (bf16[512,11,128]{2,0,1:T(8,128)(2,1)}, bf16[512,11,128]{2,0,1:T(8,128)(2,1)}, u32[]{:S(2)}, u32[]{:S(2)}) collective-permute-start(bf16[512,11,128]{2,0,1:T(8,128)(2,1)} %copy.19), channel_id=1, source_target_pairs={{0,4},{4,8},{8,12},{12,16},{16,20},{20,24},{24,28},{28,32},{32,36}... | collective-permute-start | bytes 4325384 | tf_op jit(solution)/shard_map/ppermute | solution.py:18
  69.9 94.7 %collective-permute-start.1 = (bf16[512,11,128]{2,0,1:T(8,128)(2,1)}, bf16[512,11,128]{2,0,1:T(8,128)(2,1)}, u32[]{:S(2)}, u32[]{:S(2)}) collective-permute-start(bf16[512,11,128]{2,0,1:T(8,128)(2,1)} %copy.19), channel_id=1, source_target_pairs={{4,0},{8,4},{12,8},{16,12},{20,16},{24,20},{28,24},{32,28},{36,32}... | collective-permute-start | bytes 4325384 | tf_op jit(solution)/shard_map/ppermute | solution.py:20
  162.1 4.8 copy-start.3
  192.7 482.2 %copy-start.4 = (f32[128,8,128]{2,1,0:T(8,128)S(1)}, f32[128,8,128]{2,1,0:T(8,128)}, u32[]{:S(2)}) copy-start(f32[128,8,128]{2,1,0:T(8,128)} %fusion.34) | copy-start | bytes 1572868
Sparse Core Ops, SparseCore 0:
  9.2 29.4 all-gather.2
where the time goes:
time: 689 us; the launch traced here: 684 us
  matrix products  325 us (47%)
  local copies, waits for them, and re-layouts  140 us (20%)
  other arithmetic  87.3 us (13%)
  blocking collectives  82.3 us (12%)
  waiting for transfers between devices  20.1 us (3%)
  starting transfers between devices  14.7 us (2%)
  between operations  13.6 us (2%)
    dot_general x27, matrix products, slot_step(): jnp.einsum('tij,trj->tri', tile, source, preferred_element_type=jnp.float32)  312 us
    gather x27, local copies, waits for them, and re-layouts, slot_step(): rows = nearby[index]  94.2 us
    all_gather x1, blocking collectives, on_device(): all_top = lax.all_gather(top_moment[None], 'leaf', axis=0, tiled=True)  72.7 us
    ge x27, other arithmetic, slot_step(): valid = column >= 0  32.9 us
    concatenate x2, other arithmetic, with_halo(): jnp.concatenate([lax.ppermute(tail, axis, [(i, (i + 1) % count) for i in...  27.6 us
    all_gather x1, waiting for transfers between devices, on_device(): arrived = lax.all_gather(charges, 'sub', axis=0, tiled=True)  19.4 us
    select_n x27, other arithmetic, slot_step(): rows = nearby[index]  19 us
    sub x27, local copies, waits for them, and re-layouts, kernel_tile(): offset = targets[:, component, :, None] - sources[:, component, None, :]  18.6 us
  transfers between devices with their start and end apart: 5, of which 1 were waited for; matrix products, arithmetic and copies ran while one was open for 5% of the time, Pallas kernels for 0%

commit v1 on v0

--- a/solution.py
+++ b/solution.py
@@ -89,7 +89,9 @@
     top_moment = jnp.einsum(
         "brc,bcp->rp", group_moments, transfer2, preferred_element_type=jnp.float32
     ).astype(jnp.bfloat16)
-    all_top = lax.all_gather(top_moment[None], "leaf", axis=0, tiled=True)
+    all_top = jnp.concatenate(
+        lax.all_to_all(jnp.stack([top_moment[None]] * lax.axis_size("leaf")), "leaf", 0, 0), axis=0
+    )
     near_boxes = with_halo(group_moments, (("leaf", 0),), group_boxes)
     top_field = far_field(all_top, far3_list, coupling3, 0).astype(jnp.bfloat16)
     box_far = far_field(near_boxes, far2_list, coupling2, (group - 1) * group_boxes)

time: 689 us -> 636 us (0.923)
  blocking collectives: 82.3 us -> 9.42 us
  starting transfers between devices: 14.7 us -> 29.5 us
    all_gather x1 -> x0, blocking collectives: 72.7 us -> none  [on_device(): all_top = lax.all_gather(top_moment[None], 'leaf', axis=0, tiled=True)]
    all_to_all x0 -> x1, starting transfers between devices: none -> 14.9 us  [on_device(): lax.all_to_all(jnp.stack([top_moment[None]] * lax.axis_size('leaf')), 'le...]
  transfers between devices with their start and end apart: 5 -> 6, of which waited for: 1 -> 2; matrix products, arithmetic and copies ran while one was open for 5% -> 6% of each run, Pallas kernels for 0% -> 0%
where the time goes in v1:
time: 636 us; the launch traced here: 630 us
  matrix products  326 us (51%)
  local copies, waits for them, and re-layouts  141 us (22%)
  other arithmetic  90.5 us (14%)
  starting transfers between devices  29.5 us (5%)
  waiting for transfers between devices  19.2 us (3%)
  between operations  13.6 us (2%)
  blocking collectives  9.42 us (1%)
    dot_general x27, matrix products, slot_step(): jnp.einsum('tij,trj->tri', tile, source, preferred_element_type=jnp.float32)  312 us
    gather x27, local copies, waits for them, and re-layouts, slot_step(): rows = nearby[index]  94.2 us
    ge x27, other arithmetic, slot_step(): valid = column >= 0  33 us
    concatenate x2, other arithmetic, with_halo(): jnp.concatenate([lax.ppermute(tail, axis, [(i, (i + 1) % count) for i in...  27.4 us
    select_n x27, other arithmetic, slot_step(): rows = nearby[index]  19 us
    sub x27, local copies, waits for them, and re-layouts, kernel_tile(): offset = targets[:, component, :, None] - sources[:, component, None, :]  18.3 us
    all_gather x1, waiting for transfers between devices, on_device(): arrived = lax.all_gather(charges, 'sub', axis=0, tiled=True)  17.2 us
    all_to_all x1, starting transfers between devices, on_device(): lax.all_to_all(jnp.stack([top_moment[None]] * lax.axis_size('leaf')), 'le...  14.9 us
  transfers between devices with their start and end apart: 6, of which 2 were waited for; matrix products, arithmetic and copies ran while one was open for 6% of the time, Pallas kernels for 0%

profile of v1, /device:TPU:1, one launch (start us, length us, event | category | flops | bytes accessed | tf_op | source)
XLA Modules:
  0.0 630.3 jit_solution(10560934962274117290)
XLA Ops:
  11.1 4.8 copy.23
  21.5 17.2 %all-gather.2.cloned.1.call-done = bf16[512,8,128]{2,1,0:T(8,128)(2,1)} async-done(((bf16[128,8,128]{2,1,0:T(8,128)(2,1)}), bf16[512,8,128]{2,1,0:T(8,128)(2,1)}) %all-gather.2.cloned.1.call-update) | async-done | bytes 1048592 | tf_op jit(solution)/shard_map/all_gather | solution.py:66
  47.0 4.5 collective-permute-start
  55.1 9.4 %all_gather.7 = bf16[64,8,64]{2,1,0:T(8,128)(2,1)S(1)} all-gather(bf16[16,8,64]{2,1,0:T(8,128)(2,1)S(1)} %fusion.10), channel_id=1, replica_groups=mesh['leaf'=64,'sub'=4] {'sub'}, dimensions={0}, use_global_device_ids=true | all-gather | bytes 81920 | tf_op jit(solution)/shard_map/all_gather | solution.py:88
  64.5 6.2 collective-permute-start.2
  75.4 14.9 %all-to-all-start = ((bf16[64,2,256]{2,1,0:T(2,128)(2,1)}), bf16[64,2,256]{2,1,0:T(2,128)(2,1)S(1)}, u32[]{:S(2)}, u32[]{:S(2)}) async-start(bf16[64,2,256]{2,1,0:T(2,128)(2,1)} %reshape.144), calls=%async_computation | async-start | bytes 131072 | tf_op jit(solution)/shard_map/all_to_all | solution.py:93
  94.8 4.2 convolution_bitcast_fusion.1
  102.3 4.4 convolution_convert_fusion
  113.9 25.6 %pad_maximum_fusion = bf16[1536,11,128]{2,1,0:T(8,128)(2,1)} fusion(bf16[512,11,128]{2,1,0:T(8,128)(2,1)S(1)} %copy.22, bf16[512,8,128]{2,1,0:T(8,128)(2,1)S(1)} %broadcast_select_fusion, bf16[512,3,128]{2,1,0:T(4,128)(2,1)S(1)} %copy-done.2, bf16[512,11,128]{2,1,0:T(8,128)(2,1)S(1)} %copy.21), kind=kLoop, calls=%fused_computation.23 | loop fusion | flops 17301504 | bytes 8650752 | tf_op jit(solution)/shard_map/concatenate | solution.py:16
  139.5 482.0 %while.11 = (s32[]{:T(128)}, f32[128,8,128]{2,1,0:T(8,128)}, s32[27,128]{1,0:T(8,128)}, s32[]{:T(128)}, bf16[1536,11,128]{2,1,0:T(8,128)(2,1)}, /*index=5*/f32[128,3,128]{2,0,1:T(8,128)S(1)}, s32[]{:T(128)}, s32[]{:T(128)}) while((s32[]{:T(128)}, f32[128,8,128]{2,1,0:T(8,128)}, s32[27,128]{1,0:T(8,128)}, s32[]{:T(128)}, ...), condition=%wide.region_2.3_spmd.clone, body=%wide.region_1.2_spmd.clone.sunk | while | flops 57067264 | bytes 3513195 | solution.py:121
  140.3 3.5 gather_fusion
  145.9 11.5 %fusion.50 = f32[128,8,128]{2,1,0:T(8,128)} fusion(f32[128,128]{1,0:T(8,128)S(1)} %bitcast.93, f32[128,128]{1,0:T(8,128)} %get-tuple-element.121, f32[128,128]{1,0:T(8,128)S(1)} %bitcast.94, f32[128,128]{1,0:T(8,128)} %get-tuple-element.123, f32[128,128]{1,0:T(8,128)S(1)} %bitcast.92, f32[128,128]{1,0:T(8,128)} %get-tuple-element.125, ...), kind=kOutput, calls=%fused_computation.7.clone.1 | convolution fusion | flops 57016320 | bytes 1704065 | tf_op jit(solution)/shard_map/while/body/eval_jaxpr/tij,trj->tri/dot_general | solution.py:117
  158.0 3.5 gather_fusion
  163.6 11.6 %fusion.50 = f32[128,8,128]{2,1,0:T(8,128)} fusion(f32[128,128]{1,0:T(8,128)S(1)} %bitcast.93, f32[128,128]{1,0:T(8,128)} %get-tuple-element.121, f32[128,128]{1,0:T(8,128)S(1)} %bitcast.94, f32[128,128]{1,0:T(8,128)} %get-tuple-element.123, f32[128,128]{1,0:T(8,128)S(1)} %bitcast.92, f32[128,128]{1,0:T(8,128)} %get-tuple-element.125, ...), kind=kOutput, calls=%fused_computation.7.clone.1 | convolution fusion | flops 57016320 | bytes 1704065 | tf_op jit(solution)/shard_map/while/body/eval_jaxpr/tij,trj->tri/dot_general | solution.py:117
  175.9 3.5 gather_fusion
  181.5 11.6 %fusion.50 = f32[128,8,128]{2,1,0:T(8,128)} fusion(f32[128,128]{1,0:T(8,128)S(1)} %bitcast.93, f32[128,128]{1,0:T(8,128)} %get-tuple-element.121, f32[128,128]{1,0:T(8,128)S(1)} %bitcast.94, f32[128,128]{1,0:T(8,128)} %get-tuple-element.123, f32[128,128]{1,0:T(8,128)S(1)} %bitcast.92, f32[128,128]{1,0:T(8,128)} %get-tuple-element.125, ...), kind=kOutput, calls=%fused_computation.7.clone.1 | convolution fusion | flops 57016320 | bytes 1704065 | tf_op jit(solution)/shard_map/while/body/eval_jaxpr/tij,trj->tri/dot_general | solution.py:117
  199.3 11.6 %fusion.50 = f32[128,8,128]{2,1,0:T(8,128)} fusion(f32[128,128]{1,0:T(8,128)S(1)} %bitcast.93, f32[128,128]{1,0:T(8,128)} %get-tuple-element.121, f32[128,128]{1,0:T(8,128)S(1)} %bitcast.94, f32[128,128]{1,0:T(8,128)} %get-tuple-element.123, f32[128,128]{1,0:T(8,128)S(1)} %bitcast.92, f32[128,128]{1,0:T(8,128)} %get-tuple-element.125, ...), kind=kOutput, calls=%fused_computation.7.clone.1 | convolution fusion | flops 57016320 | bytes 1704065 | tf_op jit(solution)/shard_map/while/body/eval_jaxpr/tij,trj->tri/dot_general | solution.py:117
  217.2 11.6 %fusion.50 = f32[128,8,128]{2,1,0:T(8,128)} fusion(f32[128,128]{1,0:T(8,128)S(1)} %bitcast.93, f32[128,128]{1,0:T(8,128)} %get-tuple-element.121, f32[128,128]{1,0:T(8,128)S(1)} %bitcast.94, f32[128,128]{1,0:T(8,128)} %get-tuple-element.123, f32[128,128]{1,0:T(8,128)S(1)} %bitcast.92, f32[128,128]{1,0:T(8,128)} %get-tuple-element.125, ...), kind=kOutput, calls=%fused_computation.7.clone.1 | convolution fusion | flops 57016320 | bytes 1704065 | tf_op jit(solution)/shard_map/while/body/eval_jaxpr/tij,trj->tri/dot_general | solution.py:117
  229.5 3.5 gather_fusion
  235.0 11.6 %fusion.50 = f32[128,8,128]{2,1,0:T(8,128)} fusion(f32[128,128]{1,0:T(8,128)S(1)} %bitcast.93, f32[128,128]{1,0:T(8,128)} %get-tuple-element.121, f32[128,128]{1,0:T(8,128)S(1)} %bitcast.94, f32[128,128]{1,0:T(8,128)} %get-tuple-element.123, f32[128,128]{1,0:T(8,128)S(1)} %bitcast.92, f32[128,128]{1,0:T(8,128)} %get-tuple-element.125, ...), kind=kOutput, calls=%fused_computation.7.clone.1 | convolution fusion | flops 57016320 | bytes 1704065 | tf_op jit(solution)/shard_map/while/body/eval_jaxpr/tij,trj->tri/dot_general | solution.py:117
  247.3 3.5 gather_fusion
  252.9 11.6 %fusion.50 = f32[128,8,128]{2,1,0:T(8,128)} fusion(f32[128,128]{1,0:T(8,128)S(1)} %bitcast.93, f32[128,128]{1,0:T(8,128)} %get-tuple-element.121, f32[128,128]{1,0:T(8,128)S(1)} %bitcast.94, f32[128,128]{1,0:T(8,128)} %get-tuple-element.123, f32[128,128]{1,0:T(8,128)S(1)} %bitcast.92, f32[128,128]{1,0:T(8,128)} %get-tuple-element.125, ...), kind=kOutput, calls=%fused_computation.7.clone.1 | convolution fusion | flops 57016320 | bytes 1704065 | tf_op jit(solution)/shard_map/while/body/eval_jaxpr/tij,trj->tri/dot_general | solution.py:117
  265.2 3.5 gather_fusion
  270.8 11.6 %fusion.50 = f32[128,8,128]{2,1,0:T(8,128)} fusion(f32[128,128]{1,0:T(8,128)S(1)} %bitcast.93, f32[128,128]{1,0:T(8,128)} %get-tuple-element.121, f32[128,128]{1,0:T(8,128)S(1)} %bitcast.94, f32[128,128]{1,0:T(8,128)} %get-tuple-element.123, f32[128,128]{1,0:T(8,128)S(1)} %bitcast.92, f32[128,128]{1,0:T(8,128)} %get-tuple-element.125, ...), kind=kOutput, calls=%fused_computation.7.clone.1 | convolution fusion | flops 57016320 | bytes 1704065 | tf_op jit(solution)/shard_map/while/body/eval_jaxpr/tij,trj->tri/dot_general | solution.py:117
  288.6 11.6 %fusion.50 = f32[128,8,128]{2,1,0:T(8,128)} fusion(f32[128,128]{1,0:T(8,128)S(1)} %bitcast.93, f32[128,128]{1,0:T(8,128)} %get-tuple-element.121, f32[128,128]{1,0:T(8,128)S(1)} %bitcast.94, f32[128,128]{1,0:T(8,128)} %get-tuple-element.123, f32[128,128]{1,0:T(8,128)S(1)} %bitcast.92, f32[128,128]{1,0:T(8,128)} %get-tuple-element.125, ...), kind=kOutput, calls=%fused_computation.7.clone.1 | convolution fusion | flops 57016320 | bytes 1704065 | tf_op jit(solution)/shard_map/while/body/eval_jaxpr/tij,trj->tri/dot_general | solution.py:117
  306.5 11.6 %fusion.50 = f32[128,8,128]{2,1,0:T(8,128)} fusion(f32[128,128]{1,0:T(8,128)S(1)} %bitcast.93, f32[128,128]{1,0:T(8,128)} %get-tuple-element.121, f32[128,128]{1,0:T(8,128)S(1)} %bitcast.94, f32[128,128]{1,0:T(8,128)} %get-tuple-element.123, f32[128,128]{1,0:T(8,128)S(1)} %bitcast.92, f32[128,128]{1,0:T(8,128)} %get-tuple-element.125, ...), kind=kOutput, calls=%fused_computation.7.clone.1 | convolution fusion | flops 57016320 | bytes 1704065 | tf_op jit(solution)/shard_map/while/body/eval_jaxpr/tij,trj->tri/dot_general | solution.py:117
  318.7 3.5 gather_fusion
  324.3 11.6 %fusion.50 = f32[128,8,128]{2,1,0:T(8,128)} fusion(f32[128,128]{1,0:T(8,128)S(1)} %bitcast.93, f32[128,128]{1,0:T(8,128)} %get-tuple-element.121, f32[128,128]{1,0:T(8,128)S(1)} %bitcast.94, f32[128,128]{1,0:T(8,128)} %get-tuple-element.123, f32[128,128]{1,0:T(8,128)S(1)} %bitcast.92, f32[128,128]{1,0:T(8,128)} %get-tuple-element.125, ...), kind=kOutput, calls=%fused_computation.7.clone.1 | convolution fusion | flops 57016320 | bytes 1704065 | tf_op jit(solution)/shard_map/while/body/eval_jaxpr/tij,trj->tri/dot_general | solution.py:117
  336.6 3.5 gather_fusion
  342.2 11.6 %fusion.50 = f32[128,8,128]{2,1,0:T(8,128)} fusion(f32[128,128]{1,0:T(8,128)S(1)} %bitcast.93, f32[128,128]{1,0:T(8,128)} %get-tuple-element.121, f32[128,128]{1,0:T(8,128)S(1)} %bitcast.94, f32[128,128]{1,0:T(8,128)} %get-tuple-element.123, f32[128,128]{1,0:T(8,128)S(1)} %bitcast.92, f32[128,128]{1,0:T(8,128)} %get-tuple-element.125, ...), kind=kOutput, calls=%fused_computation.7.clone.1 | convolution fusion | flops 57016320 | bytes 1704065 | tf_op jit(solution)/shard_map/while/body/eval_jaxpr/tij,trj->tri/dot_general | solution.py:117
  354.5 3.5 gather_fusion
  360.0 11.6 %fusion.50 = f32[128,8,128]{2,1,0:T(8,128)} fusion(f32[128,128]{1,0:T(8,128)S(1)} %bitcast.93, f32[128,128]{1,0:T(8,128)} %get-tuple-element.121, f32[128,128]{1,0:T(8,128)S(1)} %bitcast.94, f32[128,128]{1,0:T(8,128)} %get-tuple-element.123, f32[128,128]{1,0:T(8,128)S(1)} %bitcast.92, f32[128,128]{1,0:T(8,128)} %get-tuple-element.125, ...), kind=kOutput, calls=%fused_computation.7.clone.1 | convolution fusion | flops 57016320 | bytes 1704065 | tf_op jit(solution)/shard_map/while/body/eval_jaxpr/tij,trj->tri/dot_general | solution.py:117
  372.3 3.5 gather_fusion
  377.9 11.6 %fusion.50 = f32[128,8,128]{2,1,0:T(8,128)} fusion(f32[128,128]{1,0:T(8,128)S(1)} %bitcast.93, f32[128,128]{1,0:T(8,128)} %get-tuple-element.121, f32[128,128]{1,0:T(8,128)S(1)} %bitcast.94, f32[128,128]{1,0:T(8,128)} %get-tuple-element.123, f32[128,128]{1,0:T(8,128)S(1)} %bitcast.92, f32[128,128]{1,0:T(8,128)} %get-tuple-element.125, ...), kind=kOutput, calls=%fused_computation.7.clone.1 | convolution fusion | flops 57016320 | bytes 1704065 | tf_op jit(solution)/shard_map/while/body/eval_jaxpr/tij,trj->tri/dot_general | solution.py:117
  395.7 11.6 %fusion.50 = f32[128,8,128]{2,1,0:T(8,128)} fusion(f32[128,128]{1,0:T(8,128)S(1)} %bitcast.93, f32[128,128]{1,0:T(8,128)} %get-tuple-element.121, f32[128,128]{1,0:T(8,128)S(1)} %bitcast.94, f32[128,128]{1,0:T(8,128)} %get-tuple-element.123, f32[128,128]{1,0:T(8,128)S(1)} %bitcast.92, f32[128,128]{1,0:T(8,128)} %get-tuple-element.125, ...), kind=kOutput, calls=%fused_computation.7.clone.1 | convolution fusion | flops 57016320 | bytes 1704065 | tf_op jit(solution)/shard_map/while/body/eval_jaxpr/tij,trj->tri/dot_general | solution.py:117
  413.6 11.6 %fusion.50 = f32[128,8,128]{2,1,0:T(8,128)} fusion(f32[128,128]{1,0:T(8,128)S(1)} %bitcast.93, f32[128,128]{1,0:T(8,128)} %get-tuple-element.121, f32[128,128]{1,0:T(8,128)S(1)} %bitcast.94, f32[128,128]{1,0:T(8,128)} %get-tuple-element.123, f32[128,128]{1,0:T(8,128)S(1)} %bitcast.92, f32[128,128]{1,0:T(8,128)} %get-tuple-element.125, ...), kind=kOutput, calls=%fused_computation.7.clone.1 | convolution fusion | flops 57016320 | bytes 1704065 | tf_op jit(solution)/shard_map/while/body/eval_jaxpr/tij,trj->tri/dot_general | solution.py:117
  431.4 11.6 %fusion.50 = f32[128,8,128]{2,1,0:T(8,128)} fusion(f32[128,128]{1,0:T(8,128)S(1)} %bitcast.93, f32[128,128]{1,0:T(8,128)} %get-tuple-element.121, f32[128,128]{1,0:T(8,128)S(1)} %bitcast.94, f32[128,128]{1,0:T(8,128)} %get-tuple-element.123, f32[128,128]{1,0:T(8,128)S(1)} %bitcast.92, f32[128,128]{1,0:T(8,128)} %get-tuple-element.125, ...), kind=kOutput, calls=%fused_computation.7.clone.1 | convolution fusion | flops 57016320 | bytes 1704065 | tf_op jit(solution)/shard_map/while/body/eval_jaxpr/tij,trj->tri/dot_general | solution.py:117
  449.3 11.6 %fusion.50 = f32[128,8,128]{2,1,0:T(8,128)} fusion(f32[128,128]{1,0:T(8,128)S(1)} %bitcast.93, f32[128,128]{1,0:T(8,128)} %get-tuple-element.121, f32[128,128]{1,0:T(8,128)S(1)} %bitcast.94, f32[128,128]{1,0:T(8,128)} %get-tuple-element.123, f32[128,128]{1,0:T(8,128)S(1)} %bitcast.92, f32[128,128]{1,0:T(8,128)} %get-tuple-element.125, ...), kind=kOutput, calls=%fused_computation.7.clone.1 | convolution fusion | flops 57016320 | bytes 1704065 | tf_op jit(solution)/shard_map/while/body/eval_jaxpr/tij,trj->tri/dot_general | solution.py:117
  461.6 3.5 gather_fusion
  467.1 11.6 %fusion.50 = f32[128,8,128]{2,1,0:T(8,128)} fusion(f32[128,128]{1,0:T(8,128)S(1)} %bitcast.93, f32[128,128]{1,0:T(8,128)} %get-tuple-element.121, f32[128,128]{1,0:T(8,128)S(1)} %bitcast.94, f32[128,128]{1,0:T(8,128)} %get-tuple-element.123, f32[128,128]{1,0:T(8,128)S(1)} %bitcast.92, f32[128,128]{1,0:T(8,128)} %get-tuple-element.125, ...), kind=kOutput, calls=%fused_computation.7.clone.1 | convolution fusion | flops 57016320 | bytes 1704065 | tf_op jit(solution)/shard_map/while/body/eval_jaxpr/tij,trj->tri/dot_general | solution.py:117
  485.0 11.6 %fusion.50 = f32[128,8,128]{2,1,0:T(8,128)} fusion(f32[128,128]{1,0:T(8,128)S(1)} %bitcast.93, f32[128,128]{1,0:T(8,128)} %get-tuple-element.121, f32[128,128]{1,0:T(8,128)S(1)} %bitcast.94, f32[128,128]{1,0:T(8,128)} %get-tuple-element.123, f32[128,128]{1,0:T(8,128)S(1)} %bitcast.92, f32[128,128]{1,0:T(8,128)} %get-tuple-element.125, ...), kind=kOutput, calls=%fused_computation.7.clone.1 | convolution fusion | flops 57016320 | bytes 1704065 | tf_op jit(solution)/shard_map/while/body/eval_jaxpr/tij,trj->tri/dot_general | solution.py:117
  502.9 11.6 %fusion.50 = f32[128,8,128]{2,1,0:T(8,128)} fusion(f32[128,128]{1,0:T(8,128)S(1)} %bitcast.93, f32[128,128]{1,0:T(8,128)} %get-tuple-element.121, f32[128,128]{1,0:T(8,128)S(1)} %bitcast.94, f32[128,128]{1,0:T(8,128)} %get-tuple-element.123, f32[128,128]{1,0:T(8,128)S(1)} %bitcast.92, f32[128,128]{1,0:T(8,128)} %get-tuple-element.125, ...), kind=kOutput, calls=%fused_computation.7.clone.1 | convolution fusion | flops 57016320 | bytes 1704065 | tf_op jit(solution)/shard_map/while/body/eval_jaxpr/tij,trj->tri/dot_general | solution.py:117
  520.7 11.6 %fusion.50 = f32[128,8,128]{2,1,0:T(8,128)} fusion(f32[128,128]{1,0:T(8,128)S(1)} %bitcast.93, f32[128,128]{1,0:T(8,128)} %get-tuple-element.121, f32[128,128]{1,0:T(8,128)S(1)} %bitcast.94, f32[128,128]{1,0:T(8,128)} %get-tuple-element.123, f32[128,128]{1,0:T(8,128)S(1)} %bitcast.92, f32[128,128]{1,0:T(8,128)} %get-tuple-element.125, ...), kind=kOutput, calls=%fused_computation.7.clone.1 | convolution fusion | flops 57016320 | bytes 1704065 | tf_op jit(solution)/shard_map/while/body/eval_jaxpr/tij,trj->tri/dot_general | solution.py:117
  538.5 11.6 %fusion.50 = f32[128,8,128]{2,1,0:T(8,128)} fusion(f32[128,128]{1,0:T(8,128)S(1)} %bitcast.93, f32[128,128]{1,0:T(8,128)} %get-tuple-element.121, f32[128,128]{1,0:T(8,128)S(1)} %bitcast.94, f32[128,128]{1,0:T(8,128)} %get-tuple-element.123, f32[128,128]{1,0:T(8,128)S(1)} %bitcast.92, f32[128,128]{1,0:T(8,128)} %get-tuple-element.125, ...), kind=kOutput, calls=%fused_computation.7.clone.1 | convolution fusion | flops 57016320 | bytes 1704065 | tf_op jit(solution)/shard_map/while/body/eval_jaxpr/tij,trj->tri/dot_general | solution.py:117
  556.4 11.6 %fusion.50 = f32[128,8,128]{2,1,0:T(8,128)} fusion(f32[128,128]{1,0:T(8,128)S(1)} %bitcast.93, f32[128,128]{1,0:T(8,128)} %get-tuple-element.121, f32[128,128]{1,0:T(8,128)S(1)} %bitcast.94, f32[128,128]{1,0:T(8,128)} %get-tuple-element.123, f32[128,128]{1,0:T(8,128)S(1)} %bitcast.92, f32[128,128]{1,0:T(8,128)} %get-tuple-element.125, ...), kind=kOutput, calls=%fused_computation.7.clone.1 | convolution fusion | flops 57016320 | bytes 1704065 | tf_op jit(solution)/shard_map/while/body/eval_jaxpr/tij,trj->tri/dot_general | solution.py:117
  574.2 11.6 %fusion.50 = f32[128,8,128]{2,1,0:T(8,128)} fusion(f32[128,128]{1,0:T(8,128)S(1)} %bitcast.93, f32[128,128]{1,0:T(8,128)} %get-tuple-element.121, f32[128,128]{1,0:T(8,128)S(1)} %bitcast.94, f32[128,128]{1,0:T(8,128)} %get-tuple-element.123, f32[128,128]{1,0:T(8,128)S(1)} %bitcast.92, f32[128,128]{1,0:T(8,128)} %get-tuple-element.125, ...), kind=kOutput, calls=%fused_computation.7.clone.1 | convolution fusion | flops 57016320 | bytes 1704065 | tf_op jit(solution)/shard_map/while/body/eval_jaxpr/tij,trj->tri/dot_general | solution.py:117
  592.1 11.6 %fusion.50 = f32[128,8,128]{2,1,0:T(8,128)} fusion(f32[128,128]{1,0:T(8,128)S(1)} %bitcast.93, f32[128,128]{1,0:T(8,128)} %get-tuple-element.121, f32[128,128]{1,0:T(8,128)S(1)} %bitcast.94, f32[128,128]{1,0:T(8,128)} %get-tuple-element.123, f32[128,128]{1,0:T(8,128)S(1)} %bitcast.92, f32[128,128]{1,0:T(8,128)} %get-tuple-element.125, ...), kind=kOutput, calls=%fused_computation.7.clone.1 | convolution fusion | flops 57016320 | bytes 1704065 | tf_op jit(solution)/shard_map/while/body/eval_jaxpr/tij,trj->tri/dot_general | solution.py:117
  609.9 11.6 %fusion.50 = f32[128,8,128]{2,1,0:T(8,128)} fusion(f32[128,128]{1,0:T(8,128)S(1)} %bitcast.93, f32[128,128]{1,0:T(8,128)} %get-tuple-element.121, f32[128,128]{1,0:T(8,128)S(1)} %bitcast.94, f32[128,128]{1,0:T(8,128)} %get-tuple-element.123, f32[128,128]{1,0:T(8,128)S(1)} %bitcast.92, f32[128,128]{1,0:T(8,128)} %get-tuple-element.125, ...), kind=kOutput, calls=%fused_computation.7.clone.1 | convolution fusion | flops 57016320 | bytes 1704065 | tf_op jit(solution)/shard_map/while/body/eval_jaxpr/tij,trj->tri/dot_general | solution.py:117
  (238 shorter events, 174.4 us)
Async XLA Ops:
  6.5 46.9 %copy-start = (bf16[128,64,128]{2,1,0:T(8,128)(2,1)S(1)}, bf16[128,64,128]{2,1,0:T(8,128)(2,1)}, u32[]{:S(2)}) copy-start(bf16[128,64,128]{2,1,0:T(8,128)(2,1)} %param.19) | copy-start | bytes 6291460
  6.5 14.4 %copy-start.5 = (s32[16,16]{1,0:T(8,128)S(1)}, s32[16,16]{1,0:T(8,128)}, u32[]{:S(2)}) copy-start(s32[16,16]{1,0:T(8,128)} %param.21) | copy-start | bytes 3076
  6.5 12.2 %copy-start.7 = (s32[1,8]{1,0:T(1,128)S(1)}, s32[1,8]{1,0:T(1,128)}, u32[]{:S(2)}) copy-start(s32[1,8]{1,0:T(1,128)} %param.24) | copy-start | bytes 100
  6.5 12.8 %copy-start.6 = (s32[512]{0:T(512)S(1)}, s32[512]{0:T(512)}, u32[]{:S(2)}) copy-start(s32[512]{0:T(512)} %param.16) | copy-start | bytes 6148
  6.5 32.1 %all-gather.2.cloned.1.call-start = ((), (), s32[]{:S(2)}) async-start(), calls=%async_computation.1 | async-start | bytes 1310720 | tf_op jit(solution)/shard_map/all_gather | solution.py:66
  43.5 11.2 %copy-start.1 = (bf16[128,64,64]{2,1,0:T(8,128)(2,1)S(1)}, bf16[128,64,64]{2,1,0:T(8,128)(2,1)}, u32[]{:S(2)}) copy-start(bf16[128,64,64]{2,1,0:T(8,128)(2,1)} %copy.23) | copy-start | bytes 3145732
  45.5 27.2 %copy-start.4 = (bf16[64,64,64]{2,1,0:T(8,128)(2,1)S(1)}, bf16[64,64,64]{2,1,0:T(8,128)(2,1)}, u32[]{:S(2)}) copy-start(bf16[64,64,64]{2,1,0:T(8,128)(2,1)} %param.23) | copy-start | bytes 1572868
  47.0 62.1 %collective-permute-start = (bf16[512,11,128]{2,0,1:T(8,128)(2,1)}, bf16[512,11,128]{2,0,1:T(8,128)(2,1)}, u32[]{:S(2)}, u32[]{:S(2)}) collective-permute-start(bf16[512,11,128]{2,0,1:T(8,128)(2,1)} %copy.19), channel_id=1, source_target_pairs={{0,4},{4,8},{8,12},{12,16},{16,20},{20,24},{24,28},{28,32},{32,36}... | collective-permute-start | bytes 4325384 | tf_op jit(solution)/shard_map/ppermute | solution.py:18
  51.6 60.0 %collective-permute-start.1 = (bf16[512,11,128]{2,0,1:T(8,128)(2,1)}, bf16[512,11,128]{2,0,1:T(8,128)(2,1)}, u32[]{:S(2)}, u32[]{:S(2)}) collective-permute-start(bf16[512,11,128]{2,0,1:T(8,128)(2,1)} %copy.19), channel_id=1, source_target_pairs={{4,0},{8,4},{12,8},{16,12},{20,16},{24,20},{28,24},{32,28},{36,32}... | collective-permute-start | bytes 4325384 | tf_op jit(solution)/shard_map/ppermute | solution.py:20
  64.5 25.7 %collective-permute-start.2 = (bf16[64,8,64]{2,1,0:T(8,128)(2,1)S(1)}, bf16[64,8,64]{2,1,0:T(8,128)(2,1)}, u32[]{:S(2)}, u32[]{:S(2)}) collective-permute-start(bf16[64,8,64]{2,1,0:T(8,128)(2,1)S(1)} %all_gather.7), channel_id=1, source_target_pairs={{0,4},{4,8},{8,12},{12,16},{16,20},{20,24},{24,28},{28,32},{32,36}... | collective-permute-start | bytes 196616 | tf_op jit(solution)/shard_map/ppermute | solution.py:18
  70.8 19.5 %collective-permute-start.3 = (bf16[64,8,64]{2,1,0:T(8,128)(2,1)S(1)}, bf16[64,8,64]{2,1,0:T(8,128)(2,1)}, u32[]{:S(2)}, u32[]{:S(2)}) collective-permute-start(bf16[64,8,64]{2,1,0:T(8,128)(2,1)S(1)} %all_gather.7), channel_id=1, source_target_pairs={{4,0},{8,4},{12,8},{16,12},{20,16},{24,20},{28,24},{32,28},{36,32}... | collective-permute-start | bytes 196616 | tf_op jit(solution)/shard_map/ppermute | solution.py:20
  75.4 25.0 %all-to-all-start = ((bf16[64,2,256]{2,1,0:T(2,128)(2,1)}), bf16[64,2,256]{2,1,0:T(2,128)(2,1)S(1)}, u32[]{:S(2)}, u32[]{:S(2)}) async-start(bf16[64,2,256]{2,1,0:T(2,128)(2,1)} %reshape.144), calls=%async_computation | async-start | bytes 131072 | tf_op jit(solution)/shard_map/all_to_all | solution.py:93
  109.1 4.8 copy-start.2
  139.5 482.0 %copy-start.3 = (f32[128,8,128]{2,1,0:T(8,128)S(1)}, f32[128,8,128]{2,1,0:T(8,128)}, u32[]{:S(2)}) copy-start(f32[128,8,128]{2,1,0:T(8,128)} %fusion.34) | copy-start | bytes 1572868
Sparse Core Ops, SparseCore 0:
  9.2 29.4 all-gather.1
